TPU v7x, 256 devices: a whole 4x4x8 slice. The times are simulated.
256 devices in a mesh: wide: 32 (over z_hi, y, x), narrow: 8 (over z_lo, core).
Axes of the slice: x: 4, y: 4, z: 8 (z_hi: 2, z_lo: 4; z = z_hi * 4 + z_lo), core: 2. Of those that a mesh axis runs over, the one named last changes fastest.
Arguments:
- tile_pool: bfloat16 [32, 1024, 768], P('wide', 'narrow'), may hold values from -96 to 96
- batch_index: int32 [32, 2048], P('wide', 'narrow'), may hold values from 0 to 127
- pair_label: int32 [32, 2048], P('wide', 'narrow'), may hold values from 0 to 255, as said below
- w_first: bfloat16 [768, 2048], P('narrow'), may hold values from -0.375 to 0.375
- w_second: bfloat16 [2048, 2048], P('narrow'), may hold values from -0.375 to 0.375
- m_first: bfloat16 [32, 768, 2048], P('wide', 'narrow'), may hold values from -0.01275776 to 0.01275776
- m_second: bfloat16 [32, 2048, 2048], P('wide', 'narrow'), may hold values from -0.0078125 to 0.0078125
- v_first: bfloat16 [32, 768, 2048], P('wide', 'narrow'), may hold values from 0.0005086263 to 0.025431315
- v_second: bfloat16 [32, 2048, 2048], P('wide', 'narrow'), may hold values from 0.00019073486 to 0.009536743
- mom_first: bfloat16 [768, 2048], P('narrow'), may hold values from -0.1796875 to 0.1796875
- mom_second: bfloat16 [2048, 2048], P('narrow'), may hold values from -0.1796875 to 0.1796875
Outputs:
- new_first: bfloat16 [768, 2048], P('narrow')
- new_second: bfloat16 [2048, 2048], P('narrow')
- mom_out_first: bfloat16 [768, 2048], P('narrow')
- mom_out_second: bfloat16 [2048, 2048], P('narrow')
Inputs may be any that keep to these rules, and one draw needn't show every extreme that they name: `batch_index`: indices count within the pool of the same site and shard. `pair_label`: each row's partner is another row of the same site and shard, counted within that shard's 256 rows, and names the row back.
All inputs are finite; a program needn't handle non-finite values.
Results may differ from a plain program's by a relative error of at most 0.0075.
Values may be sent and summed in bfloat16 or wider, within the bound.
A program may use at most 128 MiB of HBM per device.

v0:
```python
import math
import jax
import jax.numpy as jnp
import numpy as np
from jax import lax
from jax.sharding import Mesh
from jax.sharding import PartitionSpec as P

PIX = 768
MID = 2048
OUT = 2048
logit_scale = 1.0 / 0.07
rate_inner = 0.2
weight_decay = 0.1
beta_first = 0.9
beta_second = 0.95
adam_eps = 1e-08
rate_outer = 0.7
momentum_coef = 0.9
WIDE = ("zh", "y", "x")
NARROW = ("zl", "c")


def adam_delta(grads, first_moment, second_moment, weights):
    moment_one = beta_first * first_moment.astype(jnp.float32) + (1.0 - beta_first) * grads
    moment_two = (
        beta_second * second_moment.astype(jnp.float32) + (1.0 - beta_second) * grads * grads
    )
    return rate_inner * (
        moment_one / (jnp.sqrt(moment_two) + adam_eps) + weight_decay * weights.astype(jnp.float32)
    )


def outer_update(delta, momentum, weights):
    velocity = momentum_coef * momentum.astype(jnp.float32) + delta
    updated = weights.astype(jnp.float32) - rate_outer * (delta + momentum_coef * velocity)
    return (updated.astype(jnp.bfloat16), velocity.astype(jnp.bfloat16))


def embed_gradient(embedded, partner):
    inverse = lax.rsqrt(jnp.sum(embedded * embedded, axis=1, keepdims=True) + OUT * 1e-06)
    unit_rows = embedded * inverse
    unit_half = unit_rows.astype(jnp.bfloat16)
    scores = logit_scale * jnp.dot(unit_half, unit_half.T, preferred_element_type=jnp.float32)
    positions = jnp.arange(embedded.shape[0], dtype=jnp.int32)
    diagonal = positions[:, None] == positions[None, :]
    scores = jnp.where(diagonal, -1e30, scores)
    highest = jnp.max(scores, axis=1, keepdims=True)
    powers = jnp.exp(scores - highest)
    softmax_rows = powers / jnp.sum(powers, axis=1, keepdims=True)
    target = (partner[:, None] == positions[None, :]).astype(jnp.float32)
    score_grad = softmax_rows - target
    paired = (score_grad + score_grad.T).astype(jnp.bfloat16)
    unit_grad = logit_scale * jnp.dot(paired, unit_half, preferred_element_type=jnp.float32)
    embed_grad = inverse * (
        unit_grad - unit_rows * jnp.sum(unit_rows * unit_grad, axis=1, keepdims=True)
    )
    return embed_grad.astype(jnp.bfloat16)


def wide_mean_update(delta, momentum, weights, axis):
    sites = lax.axis_size(WIDE)
    piece = delta.shape[axis] // sites
    got = lax.all_to_all(delta, WIDE, axis, axis, tiled=True)
    got = jnp.moveaxis(got, axis, 0).reshape((sites, piece) + (delta.shape[1 - axis],))
    mean = jnp.moveaxis(jnp.sum(got, axis=0), 0, axis) / sites
    start = lax.axis_index(WIDE) * piece
    mom_piece = lax.dynamic_slice_in_dim(momentum, start, piece, axis=axis)
    w_piece = lax.dynamic_slice_in_dim(weights, start, piece, axis=axis)
    new_piece, vel_piece = outer_update(mean, mom_piece, w_piece)
    both = jnp.stack([new_piece, vel_piece], axis=0)
    spread = jnp.broadcast_to(both[None], (sites,) + both.shape)
    back = lax.all_to_all(spread, WIDE, 0, 0, tiled=True)
    back = jnp.moveaxis(back, 0, 1 + axis)
    shape = list(delta.shape)
    back = back.reshape([2] + shape)
    return (back[0], back[1])


def shards(
    tile_pool,
    batch_index,
    pair_label,
    w_first,
    w_second,
    m_first,
    m_second,
    v_first,
    v_second,
    mom_first,
    mom_second,
):
    inputs = jnp.take(tile_pool[0], batch_index[0], axis=0)
    partner = pair_label[0]
    scale_one = 1.0 / math.sqrt(PIX)
    scale_two = 1.0 / math.sqrt(MID)
    hidden = (
        jnp.dot(
            inputs,
            lax.all_gather(w_first, NARROW, axis=0, tiled=True),
            preferred_element_type=jnp.float32,
        )
        * scale_one
    )
    active_full, gelu_back = jax.vjp(jax.nn.gelu, hidden)
    active = active_full.astype(jnp.bfloat16)
    second_whole = lax.all_gather(w_second, NARROW, axis=0, tiled=True)
    embedded = jnp.dot(active, second_whole, preferred_element_type=jnp.float32) * scale_two
    embed_half = embed_gradient(embedded, partner)
    active_grad = scale_two * jnp.dot(
        embed_half, second_whole.T, preferred_element_type=jnp.float32
    )
    hidden_half = gelu_back(active_grad)[0].astype(jnp.bfloat16)
    grad_first = lax.psum_scatter(
        (scale_one * jnp.dot(inputs.T, hidden_half, preferred_element_type=jnp.float32)).astype(
            jnp.bfloat16
        ),
        NARROW,
        scatter_dimension=0,
        tiled=True,
    ).astype(jnp.float32)
    delta_first = adam_delta(grad_first, m_first[0], v_first[0], w_first)
    new_first, vel_first = wide_mean_update(delta_first, mom_first, w_first, 1)
    term_second = (
        scale_two * jnp.dot(active.T, embed_half, preferred_element_type=jnp.float32)
    ).astype(jnp.bfloat16)
    halves = []
    cols = term_second.shape[1] // 2
    for h in range(2):
        part = slice(h * cols, (h + 1) * cols)
        grad_part = lax.psum_scatter(
            term_second[:, part], NARROW, scatter_dimension=0, tiled=True
        ).astype(jnp.float32)
        delta_part = adam_delta(
            grad_part, m_second[0][:, part], v_second[0][:, part], w_second[:, part]
        )
        halves.append(wide_mean_update(delta_part, mom_second[:, part], w_second[:, part], 0))
    new_second = jnp.concatenate([halves[0][0], halves[1][0]], axis=1)
    vel_second = jnp.concatenate([halves[0][1], halves[1][1]], axis=1)
    return (new_first, new_second, vel_first, vel_second)


def solution(mesh):
    zh, y, x = (2, 4, 4)
    devices = np.asarray(mesh.devices)
    wide, narrow = devices.shape
    sub = Mesh(devices.reshape(zh, y, x, narrow // 2, 2), WIDE + NARROW)
    site = P(WIDE, NARROW, None)
    rows = P(NARROW, None)
    return jax.shard_map(
        shards,
        mesh=sub,
        in_specs=(
            site,
            P(WIDE, NARROW),
            P(WIDE, NARROW),
            rows,
            rows,
            site,
            site,
            site,
            site,
            rows,
            rows,
        ),
        out_specs=(rows, rows, rows, rows),
        check_vma=False,
    )
```

profile of v0, /device:TPU:64, one launch (start us, length us, event | category | flops | bytes accessed | tf_op | source)
XLA Modules:
  0.0 523.8 jit_solution(6939493928089359772)
XLA Ops:
  9.4 1.2 gather_fusion
  10.6 42.6 %all-gather.3.cloned.1.call-done = bf16[768,2048]{1,0:T(8,128)(2,1)} async-done(((bf16[96,2048]{1,0:T(8,128)(2,1)}), bf16[768,2048]{1,0:T(8,128)(2,1)}) %all-gather.3.cloned.1.call-update) | async-done | bytes 3145744 | tf_op jit(solution)/shard_map/all_gather | solution.py:100
  53.2 4.4 convolution_multiply_fusion.1
  57.6 91.0 %all-gather.5.cloned.1.call-done = bf16[2048,2048]{1,0:T(8,128)(2,1)} async-done(((bf16[256,2048]{1,0:T(8,128)(2,1)}), bf16[2048,2048]{1,0:T(8,128)(2,1)}) %all-gather.5.cloned.1.call-update) | async-done | bytes 8388624 | tf_op jit(solution)/shard_map/all_gather | solution.py:107
  148.6 6.7 %multiply_reduce_fusion.1 = (f32[256]{0:T(256)S(1)}, f32[256,2048]{1,0:T(8,128)S(1)}) fusion(bf16[2048,2048]{1,0:T(8,128)(2,1)} %all-gather.5.cloned.1.call-done, f32[256,2048]{1,0:T(8,128)} %convolution_multiply_fusion.1), kind=kOutput, calls=%fused_computation.17 | convolution fusion | flops 2153774848 | bytes 12583936 | tf_op jit(solution)/shard_map/dot_general | solution.py:108
  157.1 1.5 multiply_convert_fusion.2
  158.6 10.1 %multiply_convert_fusion.1 = bf16[768,2048]{1,0:T(8,128)(2,1)} fusion(f32[256,2048]{1,0:T(8,128)} %convolution_multiply_fusion.1, bf16[256,2048]{1,0:T(8,128)(2,1)} %multiply_convert_fusion.2, bf16[2048,2048]{1,0:T(8,128)(2,1)} %all-gather.5.cloned.1.call-done, bf16[256,768]{1,0:T(8,128)(2,1)S(1)} %gather_fusion, pred[256]{0:T(512)(128)(4,1)S(1)} %compare_and_fusion), kind=kOutput, calls=%fused_computation.2 | convolution fusion | flops 2967142400 | bytes 15073536 | tf_op jit(solution)/shard_map/dot_general | solution.py:115
  169.1 1.3 copy-done.4
  170.7 3.0 multiply_convert_fusion
  173.6 3.8 fusion.77
  178.0 34.6 %reduce-scatter.4.cloned.1.call-done = bf16[96,2048]{1,0:T(8,128)(2,1)} async-done(((bf16[768,2048]{1,0:T(8,128)(2,1)}), bf16[96,2048]{1,0:T(8,128)(2,1)}) %reduce-scatter.4.cloned.1.call-update) | async-done | bytes 393232 | tf_op jit(solution)/shard_map/reduce_scatter | solution.py:114
  212.7 1.6 fusion.33
  214.3 1.3 copy.23
  215.6 9.9 %all-to-all-start = ((f32[96,32,64]{0,2,1:T(8,128)}), f32[96,32,64]{0,2,1:T(8,128)S(1)}, u32[]{:S(2)}, u32[]{:S(2)}) async-start(f32[96,32,64]{0,2,1:T(8,128)} %bitcast.8), calls=%async_computation.1 | async-start | bytes 2097152 | tf_op jit(solution)/shard_map/all_to_all | solution.py:64
  225.6 66.0 %reduce-scatter.6.cloned.1.call-done = bf16[256,1024]{1,0:T(8,128)(2,1)} async-done(((bf16[2048,1024]{1,0:T(8,128)(2,1)}), bf16[256,1024]{1,0:T(8,128)(2,1)}) %reduce-scatter.6.cloned.1.call-update) | async-done | bytes 524304 | tf_op jit(solution)/shard_map/reduce_scatter | solution.py:131
  291.5 54.9 %reduce-scatter.8.cloned.1.call-done = bf16[256,1024]{1,0:T(8,128)(2,1)} async-done(((bf16[2048,1024]{1,0:T(8,128)(2,1)}), bf16[256,1024]{1,0:T(8,128)(2,1)}) %reduce-scatter.8.cloned.1.call-update) | async-done | bytes 524304 | tf_op jit(solution)/shard_map/reduce_scatter | solution.py:131
  346.5 4.4 fusion.11
  351.9 42.4 %all_to_all.45 = f32[32,8,1024]{2,1,0:T(8,128)S(1)} all-to-all(f32[32,8,1024]{2,1,0:T(8,128)S(1)} %get-tuple-element.14), channel_id=1, replica_groups=mesh['zh'=2,'y'=4,'x'=4,'zl'=4,'c'=2] {'zh','y','x'}, dimensions={0} | all-to-all | bytes 2097152 | tf_op jit(solution)/shard_map/all_to_all | solution.py:64
  394.3 4.7 all-to-all-start.4
  400.5 1.4 constant_dynamic-slice_fusion.1
  401.9 1.4 copy.27
  403.4 1.3 bitcast_reduce_fusion
  406.0 20.2 %all-to-all-done.4 = f32[32,8,1024]{2,1,0:T(8,128)S(1)} async-done(((f32[32,8,1024]{2,1,0:T(8,128)}), f32[32,8,1024]{2,1,0:T(8,128)S(1)}, u32[]{:S(2)}, u32[]{:S(2)}) %all-to-all-start.4) | async-done | bytes 1048608 | tf_op jit(solution)/shard_map/all_to_all | solution.py:64
  426.2 2.0 broadcast_in_dim.23
  428.2 4.7 all-to-all-start.1
  436.2 21.0 %all-to-all-done.1 = bf16[32,2,96,64]{2,3,1,0:T(8,128)(2,1)} async-done(((bf16[32,2,96,64]{2,3,1,0:T(8,128)(2,1)}), bf16[32,2,96,64]{2,3,1,0:T(8,128)(2,1)}, u32[]{:S(2)}, u32[]{:S(2)}) %all-to-all-start.1) | async-done | bytes 786464 | tf_op jit(solution)/shard_map/all_to_all | solution.py:73
  457.1 1.1 broadcast_in_dim.25
  458.2 4.4 all-to-all-start.5
  462.7 22.9 %all-to-all-done.5 = bf16[32,2,8,1024]{3,2,1,0:T(8,128)(2,1)S(1)} async-done(((bf16[32,2,8,1024]{3,2,1,0:T(8,128)(2,1)}), bf16[32,2,8,1024]{3,2,1,0:T(8,128)(2,1)S(1)}, u32[]{:S(2)}, u32[]{:S(2)}) %all-to-all-start.5) | async-done | bytes 1048608 | tf_op jit(solution)/shard_map/all_to_all | solution.py:73
  486.7 4.9 all-to-all-start.3
  491.6 1.3 fusion.78
  494.9 20.2 %all-to-all-done.3 = bf16[32,2,8,1024]{3,2,1,0:T(8,128)(2,1)S(1)} async-done(((bf16[32,2,8,1024]{3,2,1,0:T(8,128)(2,1)}), bf16[32,2,8,1024]{3,2,1,0:T(8,128)(2,1)S(1)}, u32[]{:S(2)}, u32[]{:S(2)}) %all-to-all-start.3) | async-done | bytes 1048608 | tf_op jit(solution)/shard_map/all_to_all | solution.py:73
  (61 shorter events, 17.4 us)
Async XLA Ops:
  7.2 391.8 %copy-start = (bf16[96,2048]{1,0:T(8,128)(2,1)S(1)}, bf16[96,2048]{1,0:T(8,128)(2,1)}, u32[]{:S(2)}) copy-start(bf16[96,2048]{1,0:T(8,128)(2,1)} %param.20) | copy-start | bytes 1179652
  7.2 2.2 copy-start.1
  7.2 46.0 %all-gather.3.cloned.1.call-start = ((), (), s32[]{:S(2)}) async-start(), calls=%async_computation.9 | async-start | bytes 3538944 | tf_op jit(solution)/shard_map/all_gather | solution.py:100
  7.9 2.7 copy-start.10
  7.9 140.7 %all-gather.5.cloned.1.call-start = ((), (), s32[]{:S(2)}) async-start(), calls=%async_computation.10 | async-start | bytes 9437184 | tf_op jit(solution)/shard_map/all_gather | solution.py:107
  8.7 204.0 %reduce-scatter.4.cloned.1.call-start = ((), (), s32[]{:S(2)}) async-start(), calls=%async_computation.11 | async-start | bytes 3538944 | tf_op jit(solution)/shard_map/reduce_scatter | solution.py:114
  155.3 1.0 copy-start.11
  168.8 1.6 copy-start.4
  168.8 1.9 copy-start.7
  168.8 122.7 %reduce-scatter.6.cloned.1.call-start = ((), (), s32[]{:S(2)}) async-start(), calls=%async_computation.12 | async-start | bytes 4718592 | tf_op jit(solution)/shard_map/reduce_scatter | solution.py:131
  177.4 169.0 %reduce-scatter.8.cloned.1.call-start = ((), (), s32[]{:S(2)}) async-start(), calls=%async_computation.13 | async-start | bytes 4718592 | tf_op jit(solution)/shard_map/reduce_scatter | solution.py:131
  177.5 35.2 %copy-start.5 = (bf16[96,2048]{1,0:T(8,128)(2,1)S(1)}, bf16[96,2048]{1,0:T(8,128)(2,1)}, u32[]{:S(2)}) copy-start(bf16[96,2048]{1,0:T(8,128)(2,1)} %param.14) | copy-start | bytes 1179652
  177.5 35.2 %copy-start.8 = (bf16[1,96,2048]{2,1,0:T(8,128)(2,1)S(1)}, bf16[1,96,2048]{2,1,0:T(8,128)(2,1)}, u32[]{:S(2)}) copy-start(bf16[1,96,2048]{2,1,0:T(8,128)(2,1)} %param.18) | copy-start | bytes 1179652
  177.5 35.2 %copy-start.9 = (bf16[1,96,2048]{2,1,0:T(8,128)(2,1)S(1)}, bf16[1,96,2048]{2,1,0:T(8,128)(2,1)}, u32[]{:S(2)}) copy-start(bf16[1,96,2048]{2,1,0:T(8,128)(2,1)} %param.16) | copy-start | bytes 1179652
  214.3 132.1 %copy-start.2 = (bf16[256,2048]{1,0:T(8,128)(2,1)S(1)}, bf16[256,2048]{1,0:T(8,128)(2,1)}, u32[]{:S(2)}) copy-start(bf16[256,2048]{1,0:T(8,128)(2,1)} %param.15) | copy-start | bytes 3145732
  215.6 135.3 %all-to-all-start = ((f32[96,32,64]{0,2,1:T(8,128)}), f32[96,32,64]{0,2,1:T(8,128)S(1)}, u32[]{:S(2)}, u32[]{:S(2)}) async-start(f32[96,32,64]{0,2,1:T(8,128)} %bitcast.8), calls=%async_computation.1 | async-start | bytes 2097152 | tf_op jit(solution)/shard_map/all_to_all | solution.py:64
  350.9 1.0 copy-start.3
  394.3 32.0 %all-to-all-start.4 = ((f32[32,8,1024]{2,1,0:T(8,128)}), f32[32,8,1024]{2,1,0:T(8,128)S(1)}, u32[]{:S(2)}, u32[]{:S(2)}) async-start(f32[32,8,1024]{2,1,0:T(8,128)} %get-tuple-element.15), calls=%async_computation.7 | async-start | bytes 2097152 | tf_op jit(solution)/shard_map/all_to_all | solution.py:64
  428.2 28.9 %all-to-all-start.1 = ((bf16[32,2,96,64]{2,3,1,0:T(8,128)(2,1)}), bf16[32,2,96,64]{2,3,1,0:T(8,128)(2,1)}, u32[]{:S(2)}, u32[]{:S(2)}) async-start(bf16[32,2,96,64]{2,3,1,0:T(8,128)(2,1)} %broadcast_in_dim.23), calls=%async_computation.2 | async-start | bytes 2097152 | tf_op jit(solution)/shard_map/all_to_all | solution.py:73
  432.9 1.6 copy-start.6
  458.2 27.4 %all-to-all-start.5 = ((bf16[32,2,8,1024]{3,2,1,0:T(8,128)(2,1)}), bf16[32,2,8,1024]{3,2,1,0:T(8,128)(2,1)S(1)}, u32[]{:S(2)}, u32[]{:S(2)}) async-start(bf16[32,2,8,1024]{3,2,1,0:T(8,128)(2,1)} %broadcast_in_dim.25), calls=%async_computation.8 | async-start | bytes 2097152 | tf_op jit(solution)/shard_map/all_to_all | solution.py:73
  486.7 28.4 %all-to-all-start.3 = ((bf16[32,2,8,1024]{3,2,1,0:T(8,128)(2,1)}), bf16[32,2,8,1024]{3,2,1,0:T(8,128)(2,1)S(1)}, u32[]{:S(2)}, u32[]{:S(2)}) async-start(bf16[32,2,8,1024]{3,2,1,0:T(8,128)(2,1)} %broadcast_in_dim.24), calls=%async_computation.5 | async-start | bytes 2097152 | tf_op jit(solution)/shard_map/all_to_all | solution.py:73
Sparse Core Ops, SparseCore 0:
  9.8 43.3 all-gather.2
  55.0 93.5 all-gather.4
  168.9 43.6 reduce-scatter.3
  215.1 76.4 reduce-scatter.5
  293.9 52.4 reduce-scatter.7
where the time goes:
time: 525 us; the launch traced here: 524 us
  waiting for transfers between devices  375 us (71%)
  blocking collectives  42.4 us (8%)
  starting transfers between devices  29.1 us (6%)
  matrix products  25.5 us (5%)
  local copies, waits for them, and re-layouts  22.6 us (4%)
  other arithmetic  15 us (3%)
  between operations  14 us (3%)
    reduce_scatter x2, waiting for transfers between devices, shards(): lax.psum_scatter(term_second[:, part], NARROW, scatter_dimension=0, tiled...  121 us
    all_gather x1, waiting for transfers between devices, shards(): second_whole = lax.all_gather(w_second, NARROW, axis=0, tiled=True)  91 us
    all_to_all x3, waiting for transfers between devices, wide_mean_update(): back = lax.all_to_all(spread, WIDE, 0, 0, tiled=True)  64.1 us
    all_gather x1, waiting for transfers between devices, shards(): lax.all_gather(w_first, NARROW, axis=0, tiled=True)  42.6 us
    all_to_all x1, blocking collectives, wide_mean_update(): got = lax.all_to_all(delta, WIDE, axis, axis, tiled=True)  42.4 us
    reduce_scatter x1, waiting for transfers between devices, shards(): lax.psum_scatter((scale_one * jnp.dot(inputs.T, hidden_half, preferred_el...  34.6 us
    all_to_all x2, waiting for transfers between devices, wide_mean_update(): got = lax.all_to_all(delta, WIDE, axis, axis, tiled=True)  20.2 us
    all_to_all x2, starting transfers between devices, wide_mean_update(): got = lax.all_to_all(delta, WIDE, axis, axis, tiled=True)  14.6 us
  transfers between devices with their start and end apart: 10, of which 9 were waited for; matrix products, arithmetic and copies ran while one was open for 6% of the time, Pallas kernels for 0%

commit v1 on v0

--- a/solution.py
+++ b/solution.py
@@ -104,7 +104,9 @@
     )
     active_full, gelu_back = jax.vjp(jax.nn.gelu, hidden)
     active = active_full.astype(jnp.bfloat16)
-    second_whole = lax.all_gather(w_second, NARROW, axis=0, tiled=True)
+    second_whole = jnp.concatenate(
+        lax.all_to_all(jnp.stack([w_second] * lax.axis_size(NARROW)), NARROW, 0, 0), axis=0
+    )
     embedded = jnp.dot(active, second_whole, preferred_element_type=jnp.float32) * scale_two
     embed_half = embed_gradient(embedded, partner)
     active_grad = scale_two * jnp.dot(

time: 525 us -> 609 us (1.16)
  waiting for transfers between devices: 375 us -> 448 us
  starting transfers between devices: 29.1 us -> 35.4 us
    all_to_all x0 -> x1, waiting for transfers between devices: none -> 92.3 us  [shards(): lax.all_to_all(jnp.stack([w_second] * lax.axis_size(NARROW)), NARROW, 0, 0)]
    all_gather x1 -> x0, waiting for transfers between devices: 91 us -> none  [shards(): second_whole = lax.all_gather(w_second, NARROW, axis=0, tiled=True)]
    all_gather x1, waiting for transfers between devices: 42.6 us -> 111 us  [shards(): lax.all_gather(w_first, NARROW, axis=0, tiled=True)]
    all_to_all x0 -> x1, starting transfers between devices: none -> 6.34 us  [shards(): lax.all_to_all(jnp.stack([w_second] * lax.axis_size(NARROW)), NARROW, 0, 0)]
  transfers between devices with their start and end apart: 10 -> 10, of which waited for: 9 -> 9; matrix products, arithmetic and copies ran while one was open for 6% -> 5% of each run, Pallas kernels for 0% -> 0%
where the time goes in v1:
time: 609 us; the launch traced here: 607 us
  waiting for transfers between devices  448 us (74%)
  blocking collectives  42.4 us (7%)
  starting transfers between devices  35.4 us (6%)
  local copies, waits for them, and re-layouts  28.3 us (5%)
  matrix products  25.4 us (4%)
  other arithmetic  14.3 us (2%)
  between operations  14 us (2%)
    reduce_scatter x2, waiting for transfers between devices, shards(): lax.psum_scatter(term_second[:, part], NARROW, scatter_dimension=0, tiled...  121 us
    all_gather x1, waiting for transfers between devices, shards(): lax.all_gather(w_first, NARROW, axis=0, tiled=True)  111 us
    all_to_all x1, waiting for transfers between devices, shards(): lax.all_to_all(jnp.stack([w_second] * lax.axis_size(NARROW)), NARROW, 0, 0)  92.3 us
    all_to_all x3, waiting for transfers between devices, wide_mean_update(): back = lax.all_to_all(spread, WIDE, 0, 0, tiled=True)  64.1 us
    all_to_all x1, blocking collectives, wide_mean_update(): got = lax.all_to_all(delta, WIDE, axis, axis, tiled=True)  42.4 us
    reduce_scatter x1, waiting for transfers between devices, shards(): lax.psum_scatter((scale_one * jnp.dot(inputs.T, hidden_half, preferred_el...  37.6 us
    all_to_all x2, waiting for transfers between devices, wide_mean_update(): got = lax.all_to_all(delta, WIDE, axis, axis, tiled=True)  20.4 us
    all_to_all x2, starting transfers between devices, wide_mean_update(): got = lax.all_to_all(delta, WIDE, axis, axis, tiled=True)  14.8 us
  transfers between devices with their start and end apart: 10, of which 9 were waited for; matrix products, arithmetic and copies ran while one was open for 5% of the time, Pallas kernels for 0%

profile of v1, /device:TPU:64, one launch (start us, length us, event | category | flops | bytes accessed | tf_op | source)
XLA Modules:
  0.0 607.5 jit_solution(4357781904285476638)
XLA Ops:
  7.2 5.6 stack.38
  12.8 6.3 %all-to-all-start = ((bf16[8,256,2048]{2,1,0:T(8,128)(2,1)}), bf16[8,256,2048]{2,1,0:T(8,128)(2,1)}, u32[]{:S(2)}, u32[]{:S(2)}) async-start(bf16[8,256,2048]{2,1,0:T(8,128)(2,1)} %stack.38), calls=%async_computation | async-start | bytes 16777216 | tf_op jit(solution)/shard_map/all_to_all | solution.py:108
  21.2 111.3 %all-gather.2.cloned.1.call-done = bf16[768,2048]{1,0:T(8,128)(2,1)} async-done(((bf16[96,2048]{1,0:T(8,128)(2,1)}), bf16[768,2048]{1,0:T(8,128)(2,1)}) %all-gather.2.cloned.1.call-update) | async-done | bytes 3145744 | tf_op jit(solution)/shard_map/all_gather | solution.py:100
  132.5 4.3 convolution_multiply_fusion.1
  136.9 92.3 %all-to-all-done = bf16[8,256,2048]{2,1,0:T(8,128)(2,1)} async-done(((bf16[8,256,2048]{2,1,0:T(8,128)(2,1)}), bf16[8,256,2048]{2,1,0:T(8,128)(2,1)}, u32[]{:S(2)}, u32[]{:S(2)}) %all-to-all-start) | async-done | bytes 8388640 | tf_op jit(solution)/shard_map/all_to_all | solution.py:108
  229.2 6.7 %multiply_reduce_fusion.1 = (f32[256]{0:T(256)S(1)}, f32[256,2048]{1,0:T(8,128)S(1)}) fusion(bf16[2048,2048]{1,0:T(8,128)(2,1)} %bitcast.5, f32[256,2048]{1,0:T(8,128)} %convolution_multiply_fusion.1), kind=kOutput, calls=%fused_computation.17 | convolution fusion | flops 2153774848 | bytes 12583936 | tf_op jit(solution)/shard_map/dot_general | solution.py:110
  237.7 1.5 multiply_convert_fusion.2
  239.2 10.2 %multiply_convert_fusion.1 = bf16[768,2048]{1,0:T(8,128)(2,1)} fusion(f32[256,2048]{1,0:T(8,128)} %convolution_multiply_fusion.1, bf16[256,2048]{1,0:T(8,128)(2,1)} %multiply_convert_fusion.2, bf16[2048,2048]{1,0:T(8,128)(2,1)} %bitcast.5, bf16[256,768]{1,0:T(8,128)(2,1)S(1)} %gather_fusion, pred[256]{0:T(512)(128)(4,1)S(1)} %compare_and_fusion), kind=kOutput, calls=%fused_computation.2 | convolution fusion | flops 2967142400 | bytes 15073536 | tf_op jit(solution)/shard_map/dot_general | solution.py:117
  249.6 1.3 copy-done.4
  251.2 3.0 multiply_convert_fusion
  254.2 3.8 fusion.77
  258.6 37.6 %reduce-scatter.4.cloned.1.call-done = bf16[96,2048]{1,0:T(8,128)(2,1)} async-done(((bf16[768,2048]{1,0:T(8,128)(2,1)}), bf16[96,2048]{1,0:T(8,128)(2,1)}) %reduce-scatter.4.cloned.1.call-update) | async-done | bytes 393232 | tf_op jit(solution)/shard_map/reduce_scatter | solution.py:116
  296.2 1.6 fusion.33
  297.8 1.3 copy.23
  299.2 10.0 %all-to-all-start.1 = ((f32[96,32,64]{0,2,1:T(8,128)}), f32[96,32,64]{0,2,1:T(8,128)S(1)}, u32[]{:S(2)}, u32[]{:S(2)}) async-start(f32[96,32,64]{0,2,1:T(8,128)} %bitcast.9), calls=%async_computation.2 | async-start | bytes 2097152 | tf_op jit(solution)/shard_map/all_to_all | solution.py:64
  309.1 65.9 %reduce-scatter.6.cloned.1.call-done = bf16[256,1024]{1,0:T(8,128)(2,1)} async-done(((bf16[2048,1024]{1,0:T(8,128)(2,1)}), bf16[256,1024]{1,0:T(8,128)(2,1)}) %reduce-scatter.6.cloned.1.call-update) | async-done | bytes 524304 | tf_op jit(solution)/shard_map/reduce_scatter | solution.py:133
  375.1 54.8 %reduce-scatter.8.cloned.1.call-done = bf16[256,1024]{1,0:T(8,128)(2,1)} async-done(((bf16[2048,1024]{1,0:T(8,128)(2,1)}), bf16[256,1024]{1,0:T(8,128)(2,1)}) %reduce-scatter.8.cloned.1.call-update) | async-done | bytes 524304 | tf_op jit(solution)/shard_map/reduce_scatter | solution.py:133
  429.9 4.4 fusion.11
  435.3 42.4 %all_to_all.50 = f32[32,8,1024]{2,1,0:T(8,128)S(1)} all-to-all(f32[32,8,1024]{2,1,0:T(8,128)S(1)} %get-tuple-element.14), channel_id=1, replica_groups=mesh['zh'=2,'y'=4,'x'=4,'zl'=4,'c'=2] {'zh','y','x'}, dimensions={0} | all-to-all | bytes 2097152 | tf_op jit(solution)/shard_map/all_to_all | solution.py:64
  477.7 4.8 all-to-all-start.5
  484.0 1.4 constant_dynamic-slice_fusion.1
  485.4 1.4 copy.27
  486.9 1.3 bitcast_reduce_fusion
  489.6 20.4 %all-to-all-done.5 = f32[32,8,1024]{2,1,0:T(8,128)S(1)} async-done(((f32[32,8,1024]{2,1,0:T(8,128)}), f32[32,8,1024]{2,1,0:T(8,128)S(1)}, u32[]{:S(2)}, u32[]{:S(2)}) %all-to-all-start.5) | async-done | bytes 1048608 | tf_op jit(solution)/shard_map/all_to_all | solution.py:64
  509.9 2.0 broadcast_in_dim.23
  511.9 4.7 all-to-all-start.2
  519.8 21.0 %all-to-all-done.2 = bf16[32,2,96,64]{2,3,1,0:T(8,128)(2,1)} async-done(((bf16[32,2,96,64]{2,3,1,0:T(8,128)(2,1)}), bf16[32,2,96,64]{2,3,1,0:T(8,128)(2,1)}, u32[]{:S(2)}, u32[]{:S(2)}) %all-to-all-start.2) | async-done | bytes 786464 | tf_op jit(solution)/shard_map/all_to_all | solution.py:73
  541.9 4.4 all-to-all-start.6
  546.4 22.9 %all-to-all-done.6 = bf16[32,2,8,1024]{3,2,1,0:T(8,128)(2,1)S(1)} async-done(((bf16[32,2,8,1024]{3,2,1,0:T(8,128)(2,1)}), bf16[32,2,8,1024]{3,2,1,0:T(8,128)(2,1)S(1)}, u32[]{:S(2)}, u32[]{:S(2)}) %all-to-all-start.6) | async-done | bytes 1048608 | tf_op jit(solution)/shard_map/all_to_all | solution.py:73
  570.3 4.9 all-to-all-start.4
  575.3 1.3 fusion.78
  578.6 20.2 %all-to-all-done.4 = bf16[32,2,8,1024]{3,2,1,0:T(8,128)(2,1)S(1)} async-done(((bf16[32,2,8,1024]{3,2,1,0:T(8,128)(2,1)}), bf16[32,2,8,1024]{3,2,1,0:T(8,128)(2,1)S(1)}, u32[]{:S(2)}, u32[]{:S(2)}) %all-to-all-start.4) | async-done | bytes 1048608 | tf_op jit(solution)/shard_map/all_to_all | solution.py:73
  (61 shorter events, 18.4 us)
Async XLA Ops:
  7.2 475.3 %copy-start = (bf16[96,2048]{1,0:T(8,128)(2,1)S(1)}, bf16[96,2048]{1,0:T(8,128)(2,1)}, u32[]{:S(2)}) copy-start(bf16[96,2048]{1,0:T(8,128)(2,1)} %param.20) | copy-start | bytes 1179652
  12.8 7.1 %copy-start.10 = (s32[1,256]{1,0:T(1,128)S(1)}, s32[1,256]{1,0:T(1,128)}, u32[]{:S(2)}) copy-start(s32[1,256]{1,0:T(1,128)} %param.12) | copy-start | bytes 3076
  12.8 216.4 %all-to-all-start = ((bf16[8,256,2048]{2,1,0:T(8,128)(2,1)}), bf16[8,256,2048]{2,1,0:T(8,128)(2,1)}, u32[]{:S(2)}, u32[]{:S(2)}) async-start(bf16[8,256,2048]{2,1,0:T(8,128)(2,1)} %stack.38), calls=%async_computation | async-start | bytes 16777216 | tf_op jit(solution)/shard_map/all_to_all | solution.py:108
  19.1 0.9 copy-start.1
  19.1 113.4 %all-gather.2.cloned.1.call-start = ((), (), s32[]{:S(2)}) async-start(), calls=%async_computation.10 | async-start | bytes 3538944 | tf_op jit(solution)/shard_map/all_gather | solution.py:100
  19.8 276.4 %reduce-scatter.4.cloned.1.call-start = ((), (), s32[]{:S(2)}) async-start(), calls=%async_computation.11 | async-start | bytes 3538944 | tf_op jit(solution)/shard_map/reduce_scatter | solution.py:116
  235.9 1.0 copy-start.11
  249.4 1.6 copy-start.4
  249.4 1.9 copy-start.7
  249.4 125.7 %reduce-scatter.6.cloned.1.call-start = ((), (), s32[]{:S(2)}) async-start(), calls=%async_computation.12 | async-start | bytes 4718592 | tf_op jit(solution)/shard_map/reduce_scatter | solution.py:133
  258.0 171.9 %reduce-scatter.8.cloned.1.call-start = ((), (), s32[]{:S(2)}) async-start(), calls=%async_computation.13 | async-start | bytes 4718592 | tf_op jit(solution)/shard_map/reduce_scatter | solution.py:133
  258.1 38.2 %copy-start.5 = (bf16[96,2048]{1,0:T(8,128)(2,1)S(1)}, bf16[96,2048]{1,0:T(8,128)(2,1)}, u32[]{:S(2)}) copy-start(bf16[96,2048]{1,0:T(8,128)(2,1)} %param.14) | copy-start | bytes 1179652
  258.1 38.1 %copy-start.8 = (bf16[1,96,2048]{2,1,0:T(8,128)(2,1)S(1)}, bf16[1,96,2048]{2,1,0:T(8,128)(2,1)}, u32[]{:S(2)}) copy-start(bf16[1,96,2048]{2,1,0:T(8,128)(2,1)} %param.18) | copy-start | bytes 1179652
  258.1 38.1 %copy-start.9 = (bf16[1,96,2048]{2,1,0:T(8,128)(2,1)S(1)}, bf16[1,96,2048]{2,1,0:T(8,128)(2,1)}, u32[]{:S(2)}) copy-start(bf16[1,96,2048]{2,1,0:T(8,128)(2,1)} %param.16) | copy-start | bytes 1179652
  297.8 132.1 %copy-start.2 = (bf16[256,2048]{1,0:T(8,128)(2,1)S(1)}, bf16[256,2048]{1,0:T(8,128)(2,1)}, u32[]{:S(2)}) copy-start(bf16[256,2048]{1,0:T(8,128)(2,1)} %param.15) | copy-start | bytes 3145732
  299.2 135.2 %all-to-all-start.1 = ((f32[96,32,64]{0,2,1:T(8,128)}), f32[96,32,64]{0,2,1:T(8,128)S(1)}, u32[]{:S(2)}, u32[]{:S(2)}) async-start(f32[96,32,64]{0,2,1:T(8,128)} %bitcast.9), calls=%async_computation.2 | async-start | bytes 2097152 | tf_op jit(solution)/shard_map/all_to_all | solution.py:64
  434.3 1.0 copy-start.3
  477.7 32.2 %all-to-all-start.5 = ((f32[32,8,1024]{2,1,0:T(8,128)}), f32[32,8,1024]{2,1,0:T(8,128)S(1)}, u32[]{:S(2)}, u32[]{:S(2)}) async-start(f32[32,8,1024]{2,1,0:T(8,128)} %get-tuple-element.15), calls=%async_computation.8 | async-start | bytes 2097152 | tf_op jit(solution)/shard_map/all_to_all | solution.py:64
  511.9 28.9 %all-to-all-start.2 = ((bf16[32,2,96,64]{2,3,1,0:T(8,128)(2,1)}), bf16[32,2,96,64]{2,3,1,0:T(8,128)(2,1)}, u32[]{:S(2)}, u32[]{:S(2)}) async-start(bf16[32,2,96,64]{2,3,1,0:T(8,128)(2,1)} %broadcast_in_dim.23), calls=%async_computation.3 | async-start | bytes 2097152 | tf_op jit(solution)/shard_map/all_to_all | solution.py:73
  516.6 1.6 copy-start.6
  541.9 27.3 %all-to-all-start.6 = ((bf16[32,2,8,1024]{3,2,1,0:T(8,128)(2,1)}), bf16[32,2,8,1024]{3,2,1,0:T(8,128)(2,1)S(1)}, u32[]{:S(2)}, u32[]{:S(2)}) async-start(bf16[32,2,8,1024]{3,2,1,0:T(8,128)(2,1)} %broadcast_in_dim.25), calls=%async_computation.9 | async-start | bytes 2097152 | tf_op jit(solution)/shard_map/all_to_all | solution.py:73
  570.3 28.4 %all-to-all-start.4 = ((bf16[32,2,8,1024]{3,2,1,0:T(8,128)(2,1)}), bf16[32,2,8,1024]{3,2,1,0:T(8,128)(2,1)S(1)}, u32[]{:S(2)}, u32[]{:S(2)}) async-start(bf16[32,2,8,1024]{3,2,1,0:T(8,128)(2,1)} %broadcast_in_dim.24), calls=%async_computation.6 | async-start | bytes 2097152 | tf_op jit(solution)/shard_map/all_to_all | solution.py:73
Sparse Core Ops, SparseCore 0:
  21.7 110.8 all-gather.1
  249.5 46.6 reduce-scatter.3
  298.8 76.2 reduce-scatter.5
  377.5 52.3 reduce-scatter.7
